TPU v7x, 32 devices: a whole 2x2x4 slice. The times are simulated.
32 devices in a mesh: dom: 8 (over z, y), rep: 4 (over x, core).
Axes of the slice: x: 2, y: 2, z: 4, core: 2. Of those that a mesh axis runs over, the one named last changes fastest.
Arguments:
- features: bfloat16 [16384, 768], P(('dom', 'rep')), may hold values from -13 to 13
- sketch_matrix: bfloat16 [768, 256], replicated, may hold values from -0.21875 to 0.21875
- tiles: bfloat16 [8, 20, 256, 256], P('dom'), may hold values from 0 to 2, as said below
- tile_dst: int32 [8, 20], P('dom'), may hold values from -1 to 7, as said below
- tile_src: int32 [8, 20], P('dom'), may hold values from 0 to 11, as said below
- halo_index: int32 [8, 1024], P('dom'), may hold values from 0 to 2047
- send_order: int32 [8, 2048], P('dom'), may hold values from 0 to 2047, each once within a row
- arrival_place: int32 [8, 2048], P('dom'), may hold values from 0 to 2047, each once within a row
Outputs:
- signals: bfloat16 [3, 256, 16384], P(None, 'rep', 'dom')
Inputs may be any that keep to these rules, and one draw needn't show every extreme that they name: `tiles`: entries are zero or positive; in slot t < 8 of every partition the tile's diagonal is positive. `tile_dst`: in every partition slot t < 8 holds t, the live slots come first and the others hold -1; some partition uses every slot and some only the first 12. `tile_src`: slot t < 12 holds t in every partition; empty slots hold 0. `halo_index`: A row may be listed for several peers and more than once. `send_order`: each row is a permutation. `arrival_place`: each row is a permutation.
All inputs are finite; a program needn't handle non-finite values.
Results may differ from a plain program's by a relative error of at most 0.0034.
Values may be sent and summed in bfloat16 or wider, within the bound.
No kernel may reach another device: no remote copies, remote signals or barrier semaphores. Data moves between devices by JAX's collectives and lax.ppermute only.
A program may use at most 64 MiB of HBM per device.

v0:
```python
import jax
import jax.numpy as jnp
from jax import lax
from jax.sharding import PartitionSpec as P


def on_device(
    features, sketch_matrix, tiles, tile_dst, tile_src, halo_index, send_order, arrival_place
):
    sketched = lax.dot_general(
        sketch_matrix, features, (((0,), (1,)), ((), ())), preferred_element_type=jnp.float32
    ).astype(jnp.bfloat16)
    hop0 = lax.all_to_all(sketched, "rep", split_axis=0, concat_axis=1, tiled=True)
    tile_set = tiles[0]
    targets = tile_dst[0]
    sources = tile_src[0]
    halo_rows = halo_index[0]
    order = send_order[0]
    place = arrival_place[0]
    channels, node_count = hop0.shape
    tile_size = tile_set.shape[-1]
    block_count = node_count // tile_size
    onehot = (targets[:, None] == jnp.arange(block_count, dtype=jnp.int32)[None, :]).astype(
        jnp.float32
    )
    row_sums = jnp.sum(tile_set, axis=2, dtype=jnp.float32)
    degree = jnp.einsum("ti,tb->bi", row_sums, onehot, precision=lax.Precision.HIGHEST).reshape(
        node_count
    )

    def combine(layer, received):
        columns = jnp.concatenate([layer, received], 1)
        blocks = columns.reshape(channels, -1, tile_size)[:, sources, :]
        products = jnp.einsum("ctj,tij->cti", blocks, tile_set, preferred_element_type=jnp.float32)
        summed = jnp.einsum("cti,tb->cbi", products, onehot, precision=lax.Precision.HIGHEST)
        summed = summed.reshape(channels, node_count)
        return (summed / degree[None, :]).astype(jnp.bfloat16)

    hop1 = combine(
        hop0, lax.all_to_all(hop0[:, halo_rows], "dom", split_axis=1, concat_axis=1, tiled=True)
    )
    hop2 = combine(
        hop1, lax.all_to_all(hop1[:, halo_rows], "dom", split_axis=1, concat_axis=1, tiled=True)
    )
    stacked = jnp.concatenate([hop0, hop1, hop2], 0)[:, order]
    arrived = lax.all_to_all(stacked, "dom", split_axis=1, concat_axis=1, tiled=True)
    placed = jnp.zeros_like(arrived).at[:, place].set(arrived)
    return placed.reshape(3, channels, node_count)


def solution(mesh):
    in_specs = (
        P(("dom", "rep"), None),
        P(),
        P("dom", None, None, None),
        P("dom", None),
        P("dom", None),
        P("dom", None),
        P("dom", None),
        P("dom", None),
    )
    out_specs = P(None, "rep", "dom")
    return jax.shard_map(
        on_device, mesh=mesh, in_specs=in_specs, out_specs=out_specs, check_vma=False
    )
```

profile of v0, /device:TPU:0, one launch (start us, length us, event | category | flops | bytes accessed | tf_op | source)
XLA Modules:
  0.0 109.8 jit_solution(15514057003822116897)
XLA Ops:
  0.0 0.0 copy-start
  0.0 1.1 %copy-done = bf16[512,768]{1,0:T(8,128)(2,1)S(1)} copy-done((bf16[512,768]{1,0:T(8,128)(2,1)S(1)}, bf16[512,768]{1,0:T(8,128)(2,1)}, u32[]{:S(2)}) %copy-start) | copy-done | bytes 786456
  1.1 2.1 %convolution_convert_fusion = bf16[256,512]{1,0:T(8,128)(2,1)} fusion(bf16[768,256]{1,0:T(8,128)(2,1)} %param.9, bf16[512,768]{1,0:T(8,128)(2,1)S(1)} %copy-done), kind=kOutput, calls=%fused_computation.17 | convolution fusion | flops 201457664 | bytes 1441792 | tf_op jit(solution)/shard_map/dot_general | solution.py:10
  3.3 4.4 %all-to-all-start = ((bf16[4,64,512]{2,1,0:T(8,128)(2,1)}), bf16[4,64,512]{2,1,0:T(8,128)(2,1)S(1)}, u32[]{:S(2)}, u32[]{:S(2)}) async-start(bf16[4,64,512]{2,1,0:T(8,128)(2,1)} %bitcast.2), calls=%async_computation | async-start | bytes 524288 | tf_op jit(solution)/shard_map/all_to_all | solution.py:13
  7.6 0.0 copy-done.10
  7.6 2.5 %convert_reduce_fusion = f32[20,256]{1,0:T(8,128)S(1)} fusion(bf16[1,20,256,256]{3,2,1,0:T(8,128)(2,1)} %param.10), kind=kLoop, calls=%fused_computation.6 | loop fusion | flops 2616320 | bytes 2641920 | tf_op jit(solution)/shard_map/reduce_sum | solution.py:26
  10.1 0.0 copy-done.8
  10.1 0.1 convolution_bitcast_fusion
  10.3 3.3 %all-to-all-done = bf16[4,64,512]{2,1,0:T(8,128)(2,1)S(1)} async-done(((bf16[4,64,512]{2,1,0:T(8,128)(2,1)}), bf16[4,64,512]{2,1,0:T(8,128)(2,1)S(1)}, u32[]{:S(2)}, u32[]{:S(2)}) %all-to-all-start) | async-done | bytes 262176 | tf_op jit(solution)/shard_map/all_to_all | solution.py:13
  13.7 0.3 copy.76
  13.9 3.2 %gather_fusion = bf16[1024,64]{1,0:T(8,128)(2,1)S(1)} fusion(bf16[64,2048]{0,1:T(8,128)(2,1)S(1)} %copy.76, s32[1024]{0:T(1024)S(1)} %broadcast_clamp_fusion.1), kind=kCustom, calls=%fused_computation | custom fusion | bytes 266240 | tf_op jit(solution)/shard_map/gather | solution.py:40
  17.2 0.8 copy.77
  17.9 6.5 %all-to-all-start.1 = ((bf16[64,8,128]{2,0,1:T(8,128)(2,1)}), bf16[64,8,128]{2,0,1:T(8,128)(2,1)S(1)}, u32[]{:S(2)}, u32[]{:S(2)}) async-start(bf16[64,8,128]{2,0,1:T(8,128)(2,1)} %copy.77), calls=%async_computation.1 | async-start | bytes 262144 | tf_op jit(solution)/shard_map/all_to_all | solution.py:40
  24.4 0.0 copy-done.11
  24.4 7.3 %all-to-all-done.1 = bf16[64,8,128]{2,0,1:T(8,128)(2,1)S(1)} async-done(((bf16[64,8,128]{2,0,1:T(8,128)(2,1)}), bf16[64,8,128]{2,0,1:T(8,128)(2,1)S(1)}, u32[]{:S(2)}, u32[]{:S(2)}) %all-to-all-start.1) | async-done | bytes 131104 | tf_op jit(solution)/shard_map/all_to_all | solution.py:40
  31.8 0.0 copy-start.1
  31.8 1.1 %pad_maximum_fusion.1 = bf16[64,3072]{1,0:T(8,128)(2,1)S(1)} fusion(bf16[64,1024]{1,0:T(8,128)(2,1)S(1)} %copy_bitcast_fusion.3, bf16[64,2048]{1,0:T(8,128)(2,1)} %bitcast.87), kind=kLoop, calls=%fused_computation.28 | loop fusion | flops 786432 | bytes 786432 | tf_op jit(solution)/shard_map/concatenate | solution.py:32
  32.9 0.8 copy.109
  33.7 2.5 %gather_fusion.1 = bf16[20,64,256]{2,1,0:T(8,128)(2,1)} fusion(bf16[64,12,256]{2,0,1:T(8,128)(2,1)} %bitcast.90, s32[1024]{0:T(1024)S(1)} %pad_clamp_fusion), kind=kCustom, calls=%fused_computation.1 | custom fusion | bytes 1310800 | tf_op jit(solution)/shard_map/gather | solution.py:33
  36.2 2.0 %fusion.8 = f32[64,20,256]{2,0,1:T(8,128)S(1)} fusion(bf16[1,20,256,256]{3,2,1,0:T(8,128)(2,1)S(1)} %copy-done.1, bf16[20,64,256]{2,1,0:T(8,128)(2,1)} %gather_fusion.1), kind=kOutput, calls=%fused_computation.15 | convolution fusion | flops 167772160 | bytes 4587520 | tf_op jit(solution)/shard_map/ctj,tij->cti/dot_general | solution.py:34
  38.1 1.3 %fusion.6 = f32[8,64,256]{2,0,1:T(8,128)S(1)} fusion(f32[64,20,256]{2,0,1:T(8,128)S(1)} %fusion.8, s32[20]{0:T(128)S(1)} %bitcast.109), kind=kOutput, calls=%fused_computation.13 | convolution fusion | flops 31457440 | bytes 1835088 | tf_op jit(solution)/shard_map/cti,tb->cbi/dot_general | solution.py:35
  39.5 0.2 copy.97
  39.6 0.0 copy-start.5
  39.7 0.7 divide_convert_fusion.1
  40.4 2.0 %copy.81 = bf16[64,2048]{0,1:T(8,128)(2,1)} copy(bf16[64,2048]{1,0:T(8,128)(2,1)} %divide_convert_fusion.1) | data formatting | bytes 524288 | tf_op jit(solution)/shard_map/convert_element_type | solution.py:37
  42.3 5.1 %gather_fusion.2 = bf16[1024,64]{1,0:T(8,128)(2,1)} fusion(bf16[64,2048]{0,1:T(8,128)(2,1)} %copy.81, s32[1024]{0:T(1024)S(1)} %broadcast_clamp_fusion.1), kind=kCustom, calls=%fused_computation.2 | custom fusion | bytes 266240 | tf_op jit(solution)/shard_map/gather | solution.py:43
  47.5 1.7 %copy.82 = bf16[64,8,128]{2,0,1:T(8,128)(2,1)} copy(bf16[64,8,128]{0,2,1:T(8,128)(2,1)} %bitcast.101) | data formatting | bytes 262144 | tf_op jit(solution)/shard_map/all_to_all | solution.py:43
  49.2 3.4 %all-to-all-start.2 = ((bf16[64,8,128]{2,0,1:T(8,128)(2,1)}), bf16[64,8,128]{2,0,1:T(8,128)(2,1)S(1)}, u32[]{:S(2)}, u32[]{:S(2)}) async-start(bf16[64,8,128]{2,0,1:T(8,128)(2,1)} %copy.82), calls=%async_computation.2 | async-start | bytes 262144 | tf_op jit(solution)/shard_map/all_to_all | solution.py:43
  52.6 0.0 copy-done.5
  52.6 7.2 %all-to-all-done.2 = bf16[64,8,128]{2,0,1:T(8,128)(2,1)S(1)} async-done(((bf16[64,8,128]{2,0,1:T(8,128)(2,1)}), bf16[64,8,128]{2,0,1:T(8,128)(2,1)S(1)}, u32[]{:S(2)}, u32[]{:S(2)}) %all-to-all-start.2) | async-done | bytes 131104 | tf_op jit(solution)/shard_map/all_to_all | solution.py:43
  59.9 1.0 pad_maximum_fusion.2
  60.9 0.8 copy.108
  61.7 2.6 %gather_fusion.3 = bf16[20,64,256]{2,1,0:T(8,128)(2,1)} fusion(bf16[64,12,256]{2,0,1:T(8,128)(2,1)} %bitcast.89, s32[1024]{0:T(1024)} %copy-done.7), kind=kCustom, calls=%fused_computation.3 | custom fusion | bytes 1310800 | tf_op jit(solution)/shard_map/gather | solution.py:33
  64.2 2.0 %fusion.11 = f32[64,20,256]{2,0,1:T(8,128)S(1)} fusion(bf16[1,20,256,256]{3,2,1,0:T(8,128)(2,1)S(1)} %copy-done.1, bf16[20,64,256]{2,1,0:T(8,128)(2,1)} %gather_fusion.3), kind=kOutput, calls=%fused_computation.16 | convolution fusion | flops 167772160 | bytes 4587520 | tf_op jit(solution)/shard_map/ctj,tij->cti/dot_general | solution.py:34
  66.3 1.3 %fusion.4 = f32[8,64,256]{2,0,1:T(8,128)S(1)} fusion(f32[64,20,256]{2,0,1:T(8,128)S(1)} %fusion.11, s32[20]{0:T(128)S(1)} %bitcast.110), kind=kOutput, calls=%fused_computation.11 | convolution fusion | flops 31457440 | bytes 1835088 | tf_op jit(solution)/shard_map/cti,tb->cbi/dot_general | solution.py:35
  67.6 0.2 copy.99
  67.8 0.1 pad_maximum_fusion
  67.9 0.5 copy.86
  68.4 7.5 %gather_fusion.4 = bf16[2048,192]{1,0:T(8,128)(2,1)S(1)} fusion(bf16[192,2048]{0,1:T(8,128)(2,1)S(1)} %copy.86, s32[2048]{0:T(1024)S(1)} %broadcast_clamp_fusion), kind=kCustom, calls=%fused_computation.4 | custom fusion | bytes 1581056 | tf_op jit(solution)/shard_map/gather | solution.py:45
  75.9 0.0 copy-start.6
  75.9 1.3 %copy.87 = bf16[192,8,256]{2,0,1:T(8,128)(2,1)} copy(bf16[192,8,256]{0,2,1:T(8,128)(2,1)S(1)} %bitcast.91) | data formatting | bytes 1572864 | tf_op jit(solution)/shard_map/all_to_all | solution.py:46
  77.2 3.5 %all-to-all-start.3 = ((bf16[192,8,256]{2,0,1:T(8,128)(2,1)}), bf16[192,8,256]{2,0,1:T(8,128)(2,1)S(1)}, u32[]{:S(2)}, u32[]{:S(2)}) async-start(bf16[192,8,256]{2,0,1:T(8,128)(2,1)} %copy.87), calls=%async_computation.3 | async-start | bytes 1572864 | tf_op jit(solution)/shard_map/all_to_all | solution.py:46
  80.8 0.0 copy-done.6
  80.8 17.5 %all-to-all-done.3 = bf16[192,8,256]{2,0,1:T(8,128)(2,1)S(1)} async-done(((bf16[192,8,256]{2,0,1:T(8,128)(2,1)}), bf16[192,8,256]{2,0,1:T(8,128)(2,1)S(1)}, u32[]{:S(2)}, u32[]{:S(2)}) %all-to-all-start.3) | async-done | bytes 786464 | tf_op jit(solution)/shard_map/all_to_all | solution.py:46
  98.3 0.1 copy.96
  98.4 0.5 copy.89
  98.9 9.6 %scatter_custom_fusion = bf16[192,2048]{0,1:T(8,128)(2,1)S(1)} fusion(s32[2048]{0:T(1024)S(1)} %bitcast.107, bf16[2048,192]{1,0:T(8,128)(2,1)S(1)} %copy.89, bf16[]{:T(256)} %constant.5.clone.1), kind=kCustom, calls=%fused_computation.24 | custom fusion | bytes 786434 | tf_op jit(solution)/shard_map/scatter | solution.py:47
  108.5 1.2 %copy.90 = bf16[192,2048]{1,0:T(8,128)(2,1)} copy(bf16[192,2048]{0,1:T(8,128)(2,1)S(1)} %scatter_custom_fusion) | data formatting | bytes 1572864 | tf_op jit(solution)/shard_map/scatter | solution.py:47
  (26 shorter events, 0.2 us)
Async XLA Ops:
  0.0 1.1 %copy-start = (bf16[512,768]{1,0:T(8,128)(2,1)S(1)}, bf16[512,768]{1,0:T(8,128)(2,1)}, u32[]{:S(2)}) copy-start(bf16[512,768]{1,0:T(8,128)(2,1)} %param.8) | copy-start | bytes 2359300
  0.0 7.6 %copy-start.10 = (s32[1,1024]{1,0:T(1,128)S(1)}, s32[1,1024]{1,0:T(1,128)}, u32[]{:S(2)}) copy-start(s32[1,1024]{1,0:T(1,128)} %param.13) | copy-start | bytes 12292
  3.3 6.9 %copy-start.8 = (s32[1,20]{1,0:T(1,128)S(1)}, s32[1,20]{1,0:T(1,128)}, u32[]{:S(2)}) copy-start(s32[1,20]{1,0:T(1,128)} %param.11) | copy-start | bytes 244
  3.3 10.4 %all-to-all-start = ((bf16[4,64,512]{2,1,0:T(8,128)(2,1)}), bf16[4,64,512]{2,1,0:T(8,128)(2,1)S(1)}, u32[]{:S(2)}, u32[]{:S(2)}) async-start(bf16[4,64,512]{2,1,0:T(8,128)(2,1)} %bitcast.2), calls=%async_computation | async-start | bytes 524288 | tf_op jit(solution)/shard_map/all_to_all | solution.py:13
  13.6 10.8 %copy-start.11 = (s32[1,20]{1,0:T(1,128)S(1)}, s32[1,20]{1,0:T(1,128)}, u32[]{:S(2)}) copy-start(s32[1,20]{1,0:T(1,128)} %param.12) | copy-start | bytes 244
  13.7 18.1 %copy-start.3 = (bf16[4,8,8,512]{3,2,0,1:T(8,128)(2,1)}, bf16[4,8,8,512]{3,2,0,1:T(8,128)(2,1)S(1)}, u32[]{:S(2)}) copy-start(bf16[4,8,8,512]{3,2,0,1:T(8,128)(2,1)S(1)} %copy.93) | copy-start | bytes 786436
  17.9 13.8 %all-to-all-start.1 = ((bf16[64,8,128]{2,0,1:T(8,128)(2,1)}), bf16[64,8,128]{2,0,1:T(8,128)(2,1)S(1)}, u32[]{:S(2)}, u32[]{:S(2)}) async-start(bf16[64,8,128]{2,0,1:T(8,128)(2,1)} %copy.77), calls=%async_computation.1 | async-start | bytes 262144 | tf_op jit(solution)/shard_map/all_to_all | solution.py:40
  24.4 11.7 %copy-start.7 = (s32[1024]{0:T(1024)}, s32[1024]{0:T(1024)S(1)}, u32[]{:S(2)}) copy-start(s32[1024]{0:T(1024)S(1)} %pad_clamp_fusion) | copy-start | bytes 12292
  31.8 4.4 %copy-start.1 = (bf16[1,20,256,256]{3,2,1,0:T(8,128)(2,1)S(1)}, bf16[1,20,256,256]{3,2,1,0:T(8,128)(2,1)}, u32[]{:S(2)}) copy-start(bf16[1,20,256,256]{3,2,1,0:T(8,128)(2,1)} %param.10) | copy-start | bytes 7864324
  39.6 13.0 %copy-start.5 = (s32[1,2048]{1,0:T(1,128)S(1)}, s32[1,2048]{1,0:T(1,128)}, u32[]{:S(2)}) copy-start(s32[1,2048]{1,0:T(1,128)} %param.14) | copy-start | bytes 24580
  49.2 10.7 %all-to-all-start.2 = ((bf16[64,8,128]{2,0,1:T(8,128)(2,1)}), bf16[64,8,128]{2,0,1:T(8,128)(2,1)S(1)}, u32[]{:S(2)}, u32[]{:S(2)}) async-start(bf16[64,8,128]{2,0,1:T(8,128)(2,1)} %copy.82), calls=%async_computation.2 | async-start | bytes 262144 | tf_op jit(solution)/shard_map/all_to_all | solution.py:43
  64.2 2.0 %copy-start.9 = (s32[1,20]{1,0:T(1,128)S(1)}, s32[1,20]{1,0:T(1,128)}, u32[]{:S(2)}) copy-start(s32[1,20]{1,0:T(1,128)} %param.11) | copy-start | bytes 244
  66.2 1.6 %copy-start.2 = (bf16[64,2048]{1,0:T(8,128)(2,1)S(1)}, bf16[64,2048]{1,0:T(8,128)(2,1)}, u32[]{:S(2)}) copy-start(bf16[64,2048]{1,0:T(8,128)(2,1)} %divide_convert_fusion.1) | copy-start | bytes 786436
  66.3 1.6 %copy-start.4 = (bf16[4,8,8,512]{3,2,0,1:T(8,128)(2,1)S(1)}, bf16[4,8,8,512]{3,2,0,1:T(8,128)(2,1)}, u32[]{:S(2)}) copy-start(bf16[4,8,8,512]{3,2,0,1:T(8,128)(2,1)} %copy-done.3) | copy-start | bytes 786436
  75.9 4.8 %copy-start.6 = (s32[1,2048]{1,0:T(1,128)S(1)}, s32[1,2048]{1,0:T(1,128)}, u32[]{:S(2)}) copy-start(s32[1,2048]{1,0:T(1,128)} %param.15) | copy-start | bytes 24580
  77.2 21.1 %all-to-all-start.3 = ((bf16[192,8,256]{2,0,1:T(8,128)(2,1)}), bf16[192,8,256]{2,0,1:T(8,128)(2,1)S(1)}, u32[]{:S(2)}, u32[]{:S(2)}) async-start(bf16[192,8,256]{2,0,1:T(8,128)(2,1)} %copy.87), calls=%async_computation.3 | async-start | bytes 1572864 | tf_op jit(solution)/shard_map/all_to_all | solution.py:46
where the time goes:
time: 111 us; the launch traced here: 110 us
  local copies, waits for them, and re-layouts  41.9 us (38%)
  waiting for transfers between devices  35.4 us (32%)
  starting transfers between devices  17.7 us (16%)
  matrix products  8.87 us (8%)
  other arithmetic  5.49 us (5%)
    all_to_all x1, waiting for transfers between devices, on_device(): lax.all_to_all(stacked, 'dom', split_axis=1, concat_axis=1, tiled=True)  17.5 us
    scatter x2, local copies, waits for them, and re-layouts, on_device(): placed = jnp.zeros_like(arrived).at[:, place].set(arrived)  10.8 us
    gather x1, local copies, waits for them, and re-layouts, on_device(): stacked = jnp.concatenate([hop0, hop1, hop2], 0)[:, order]  7.5 us
    all_to_all x1, waiting for transfers between devices, on_device(): lax.all_to_all(hop0[:, halo_rows], 'dom', split_axis=1, concat_axis=1, ti...  7.3 us
    all_to_all x1, waiting for transfers between devices, on_device(): lax.all_to_all(hop1[:, halo_rows], 'dom', split_axis=1, concat_axis=1, ti...  7.24 us
    all_to_all x1, starting transfers between devices, on_device(): lax.all_to_all(hop0[:, halo_rows], 'dom', split_axis=1, concat_axis=1, ti...  6.46 us
    gather x1, local copies, waits for them, and re-layouts, on_device(): hop1[:, halo_rows]  5.14 us
    gather x2, local copies, waits for them, and re-layouts, combine(): blocks = columns.reshape(channels, -1, tile_size)[:, sources, :]  5.03 us
  transfers between devices with their start and end apart: 4, of which 4 were waited for; matrix products, arithmetic and copies ran while one was open for 2% of the time, Pallas kernels for 0%

commit v1 on v0

--- a/solution.py
+++ b/solution.py
@@ -43,7 +43,10 @@
         hop1, lax.all_to_all(hop1[:, halo_rows], "dom", split_axis=1, concat_axis=1, tiled=True)
     )
     stacked = jnp.concatenate([hop0, hop1, hop2], 0)[:, order]
-    arrived = lax.all_to_all(stacked, "dom", split_axis=1, concat_axis=1, tiled=True)
+    answer_spots = lambda patch: jnp.concatenate(
+        lax.all_to_all(jnp.stack(jnp.split(patch, lax.axis_size("dom"), 1)), "dom", 0, 0), 1
+    )
+    arrived = answer_spots(stacked)
     placed = jnp.zeros_like(arrived).at[:, place].set(arrived)
     return placed.reshape(3, channels, node_count)
 

time: 111 us -> 118 us (1.063)
  local copies, waits for them, and re-layouts: 41.9 us -> 49.2 us
  other arithmetic: 5.49 us -> 4.3 us
    all_to_all x2, local copies, waits for them, and re-layouts: 0.29 us -> 3.78 us  [on_device(): lax.all_to_all(sketched, 'rep', split_axis=0, concat_axis=1, tiled=True)]
    all_to_all x1, waiting for transfers between devices: 3.34 us -> 5.95 us  [on_device(): lax.all_to_all(sketched, 'rep', split_axis=0, concat_axis=1, tiled=True)]
    gather x1, local copies, waits for them, and re-layouts: 3.21 us -> 5.17 us  [on_device(): hop0[:, halo_rows]]
    all_to_all x3 -> x0, local copies, waits for them, and re-layouts: 1.85 us -> none  [on_device(): lax.all_to_all(stacked, 'dom', split_axis=1, concat_axis=1, tiled=True)]
    reduce_sum x1, other arithmetic: 2.49 us -> 0.75 us  [on_device(): row_sums = jnp.sum(tile_set, axis=2, dtype=jnp.float32)]
    another operation x0 -> x2, local copies, waits for them, and re-layouts: none -> 1.27 us  [on_device(): jnp.stack(jnp.split(patch, lax.axis_size('dom'), 1))]
  transfers between devices with their start and end apart: 4 -> 4, of which waited for: 4 -> 4; matrix products, arithmetic and copies ran while one was open for 2% -> 1% of each run, Pallas kernels for 0% -> 0%
where the time goes in v1:
time: 118 us; the launch traced here: 117 us
  local copies, waits for them, and re-layouts  49.2 us (42%)
  waiting for transfers between devices  36.5 us (31%)
  starting transfers between devices  17.6 us (15%)
  matrix products  8.87 us (8%)
  other arithmetic  4.3 us (4%)
    all_to_all x1, waiting for transfers between devices, on_device(): lax.all_to_all(jnp.stack(jnp.split(patch, lax.axis_size('dom'), 1)), 'dom...  17.5 us
    scatter x2, local copies, waits for them, and re-layouts, on_device(): placed = jnp.zeros_like(arrived).at[:, place].set(arrived)  10.8 us
    gather x1, local copies, waits for them, and re-layouts, on_device(): stacked = jnp.concatenate([hop0, hop1, hop2], 0)[:, order]  7.5 us
    all_to_all x1, waiting for transfers between devices, on_device(): lax.all_to_all(hop1[:, halo_rows], 'dom', split_axis=1, concat_axis=1, ti...  6.56 us
    all_to_all x1, starting transfers between devices, on_device(): lax.all_to_all(hop0[:, halo_rows], 'dom', split_axis=1, concat_axis=1, ti...  6.45 us
    all_to_all x1, waiting for transfers between devices, on_device(): lax.all_to_all(hop0[:, halo_rows], 'dom', split_axis=1, concat_axis=1, ti...  6.44 us
    all_to_all x1, waiting for transfers between devices, on_device(): lax.all_to_all(sketched, 'rep', split_axis=0, concat_axis=1, tiled=True)  5.95 us
    gather x1, local copies, waits for them, and re-layouts, on_device(): hop0[:, halo_rows]  5.17 us
  transfers between devices with their start and end apart: 4, of which 4 were waited for; matrix products, arithmetic and copies ran while one was open for 1% of the time, Pallas kernels for 0%

profile of v1, /device:TPU:0, one launch (start us, length us, event | category | flops | bytes accessed | tf_op | source)
XLA Modules:
  0.0 116.8 jit_solution(15374844775916884746)
XLA Ops:
  0.0 0.0 copy-start
  0.0 1.1 copy-done
  1.1 2.1 %convolution_convert_fusion = bf16[256,512]{1,0:T(8,128)(2,1)} fusion(bf16[768,256]{1,0:T(8,128)(2,1)} %param.9, bf16[512,768]{1,0:T(8,128)(2,1)S(1)} %copy-done), kind=kOutput, calls=%fused_computation.17 | convolution fusion | flops 201457664 | bytes 1441792 | tf_op jit(solution)/shard_map/dot_general | solution.py:10
  3.3 4.2 %all-to-all-start = ((bf16[4,64,512]{2,1,0:T(8,128)(2,1)}), bf16[4,64,512]{2,1,0:T(8,128)(2,1)S(1)}, u32[]{:S(2)}, u32[]{:S(2)}) async-start(bf16[4,64,512]{2,1,0:T(8,128)(2,1)} %bitcast.2), calls=%async_computation | async-start | bytes 524288 | tf_op jit(solution)/shard_map/all_to_all | solution.py:13
  7.5 0.0 copy-done.10
  7.5 0.0 copy-done.11
  7.5 0.0 copy-start.6
  7.5 5.9 %all-to-all-done = bf16[4,64,512]{2,1,0:T(8,128)(2,1)S(1)} async-done(((bf16[4,64,512]{2,1,0:T(8,128)(2,1)}), bf16[4,64,512]{2,1,0:T(8,128)(2,1)S(1)}, u32[]{:S(2)}, u32[]{:S(2)}) %all-to-all-start) | async-done | bytes 262176 | tf_op jit(solution)/shard_map/all_to_all | solution.py:13
  13.5 0.7 copy-done.4
  14.2 1.8 %copy.93 = bf16[4,8,8,512]{3,2,0,1:T(8,128)(2,1)} copy(bf16[4,8,8,512]{3,2,1,0:T(8,128)(2,1)} %bitcast.138) | data formatting | bytes 524288 | tf_op jit(solution)/shard_map/all_to_all | solution.py:13
  16.0 2.0 %copy.76 = bf16[64,2048]{0,1:T(8,128)(2,1)} copy(bf16[64,2048]{1,0:T(8,128)(2,1)} %bitcast.117) | data formatting | bytes 524288 | tf_op jit(solution)/shard_map/all_to_all | solution.py:13
  18.0 5.2 %gather_fusion = bf16[1024,64]{1,0:T(8,128)(2,1)} fusion(bf16[64,2048]{0,1:T(8,128)(2,1)} %copy.76, s32[1024]{0:T(1024)S(1)} %get-tuple-element.6), kind=kCustom, calls=%fused_computation | custom fusion | bytes 266240 | tf_op jit(solution)/shard_map/gather | solution.py:40
  23.2 1.7 %copy.77 = bf16[64,8,128]{2,0,1:T(8,128)(2,1)} copy(bf16[64,8,128]{0,2,1:T(8,128)(2,1)} %bitcast.140) | data formatting | bytes 262144 | tf_op jit(solution)/shard_map/all_to_all | solution.py:40
  24.9 6.5 %all-to-all-start.1 = ((bf16[64,8,128]{2,0,1:T(8,128)(2,1)}), bf16[64,8,128]{2,0,1:T(8,128)(2,1)S(1)}, u32[]{:S(2)}, u32[]{:S(2)}) async-start(bf16[64,8,128]{2,0,1:T(8,128)(2,1)} %copy.77), calls=%async_computation.1 | async-start | bytes 262144 | tf_op jit(solution)/shard_map/all_to_all | solution.py:40
  31.4 0.0 copy-done.1
  31.4 0.7 convert_reduce_fusion
  32.1 0.1 convolution_bitcast_fusion
  32.3 6.4 %all-to-all-done.1 = bf16[64,8,128]{2,0,1:T(8,128)(2,1)S(1)} async-done(((bf16[64,8,128]{2,0,1:T(8,128)(2,1)}), bf16[64,8,128]{2,0,1:T(8,128)(2,1)S(1)}, u32[]{:S(2)}, u32[]{:S(2)}) %all-to-all-start.1) | async-done | bytes 131104 | tf_op jit(solution)/shard_map/all_to_all | solution.py:40
  38.7 1.0 pad_maximum_fusion.1
  39.7 0.8 copy.109
  40.5 2.5 %gather_fusion.1 = bf16[20,64,256]{2,1,0:T(8,128)(2,1)} fusion(bf16[64,12,256]{2,0,1:T(8,128)(2,1)} %bitcast.120, s32[1024]{0:T(1024)S(1)} %get-tuple-element.5), kind=kCustom, calls=%fused_computation.1 | custom fusion | bytes 1310800 | tf_op jit(solution)/shard_map/gather | solution.py:33
  42.9 2.0 %fusion.8 = f32[64,20,256]{2,0,1:T(8,128)S(1)} fusion(bf16[1,20,256,256]{3,2,1,0:T(8,128)(2,1)S(1)} %copy-done.1, bf16[20,64,256]{2,1,0:T(8,128)(2,1)} %gather_fusion.1), kind=kOutput, calls=%fused_computation.15 | convolution fusion | flops 167772160 | bytes 4587520 | tf_op jit(solution)/shard_map/ctj,tij->cti/dot_general | solution.py:34
  45.0 1.3 %fusion.6 = f32[8,64,256]{2,0,1:T(8,128)S(1)} fusion(f32[64,20,256]{2,0,1:T(8,128)S(1)} %fusion.8, s32[20]{0:T(128)S(1)} %bitcast.147), kind=kOutput, calls=%fused_computation.13 | convolution fusion | flops 31457440 | bytes 1835088 | tf_op jit(solution)/shard_map/cti,tb->cbi/dot_general | solution.py:35
  46.3 0.2 copy.97
  46.5 0.7 divide_convert_fusion.1
  47.2 2.0 %copy.81 = bf16[64,2048]{0,1:T(8,128)(2,1)} copy(bf16[64,2048]{1,0:T(8,128)(2,1)} %divide_convert_fusion.1) | data formatting | bytes 524288 | tf_op jit(solution)/shard_map/convert_element_type | solution.py:37
  49.2 5.2 %gather_fusion.2 = bf16[1024,64]{1,0:T(8,128)(2,1)} fusion(bf16[64,2048]{0,1:T(8,128)(2,1)} %copy.81, s32[1024]{0:T(1024)S(1)} %get-tuple-element.6), kind=kCustom, calls=%fused_computation.2 | custom fusion | bytes 266240 | tf_op jit(solution)/shard_map/gather | solution.py:43
  54.3 1.7 %copy.82 = bf16[64,8,128]{2,0,1:T(8,128)(2,1)} copy(bf16[64,8,128]{0,2,1:T(8,128)(2,1)} %bitcast.139) | data formatting | bytes 262144 | tf_op jit(solution)/shard_map/all_to_all | solution.py:43
  56.1 3.4 %all-to-all-start.2 = ((bf16[64,8,128]{2,0,1:T(8,128)(2,1)}), bf16[64,8,128]{2,0,1:T(8,128)(2,1)S(1)}, u32[]{:S(2)}, u32[]{:S(2)}) async-start(bf16[64,8,128]{2,0,1:T(8,128)(2,1)} %copy.82), calls=%async_computation.2 | async-start | bytes 262144 | tf_op jit(solution)/shard_map/all_to_all | solution.py:43
  59.4 0.7 compare_select_fusion
  60.2 6.6 %all-to-all-done.2 = bf16[64,8,128]{2,0,1:T(8,128)(2,1)S(1)} async-done(((bf16[64,8,128]{2,0,1:T(8,128)(2,1)}), bf16[64,8,128]{2,0,1:T(8,128)(2,1)S(1)}, u32[]{:S(2)}, u32[]{:S(2)}) %all-to-all-start.2) | async-done | bytes 131104 | tf_op jit(solution)/shard_map/all_to_all | solution.py:43
  66.7 1.0 pad_maximum_fusion.2
  67.7 0.8 copy.108
  68.5 2.6 %gather_fusion.3 = bf16[20,64,256]{2,1,0:T(8,128)(2,1)} fusion(bf16[64,12,256]{2,0,1:T(8,128)(2,1)} %bitcast.121, s32[1024]{0:T(1024)} %copy-done.6), kind=kCustom, calls=%fused_computation.3 | custom fusion | bytes 1310800 | tf_op jit(solution)/shard_map/gather | solution.py:33
  71.1 2.0 %fusion.11 = f32[64,20,256]{2,0,1:T(8,128)S(1)} fusion(bf16[1,20,256,256]{3,2,1,0:T(8,128)(2,1)S(1)} %copy-done.1, bf16[20,64,256]{2,1,0:T(8,128)(2,1)} %gather_fusion.3), kind=kOutput, calls=%fused_computation.16 | convolution fusion | flops 167772160 | bytes 4587520 | tf_op jit(solution)/shard_map/ctj,tij->cti/dot_general | solution.py:34
  73.1 1.3 %fusion.4 = f32[8,64,256]{2,0,1:T(8,128)S(1)} fusion(f32[64,20,256]{2,0,1:T(8,128)S(1)} %fusion.11, s32[20]{0:T(128)S(1)} %bitcast.148), kind=kOutput, calls=%fused_computation.11 | convolution fusion | flops 31457440 | bytes 1835088 | tf_op jit(solution)/shard_map/cti,tb->cbi/dot_general | solution.py:35
  74.4 0.2 copy.99
  74.7 0.1 pad_maximum_fusion
  74.8 0.5 copy.86
  75.3 7.5 %gather_fusion.4 = bf16[2048,192]{1,0:T(8,128)(2,1)S(1)} fusion(bf16[192,2048]{0,1:T(8,128)(2,1)S(1)} %copy.86, s32[2048]{0:T(1024)S(1)} %broadcast_clamp_fusion), kind=kCustom, calls=%fused_computation.4 | custom fusion | bytes 1581056 | tf_op jit(solution)/shard_map/gather | solution.py:45
  82.9 0.0 copy-start.5
  83.0 1.3 %copy.87 = bf16[8,192,256]{2,1,0:T(8,128)(2,1)} copy(bf16[8,192,256]{1,2,0:T(8,128)(2,1)S(1)} %fusion.18) | data formatting | bytes 1572864 | tf_op jit(solution)/shard_map/stack | solution.py:47
  84.2 3.5 %all-to-all-start.3 = ((bf16[8,192,256]{2,1,0:T(8,128)(2,1)}), bf16[8,192,256]{2,1,0:T(8,128)(2,1)S(1)}, u32[]{:S(2)}, u32[]{:S(2)}) async-start(bf16[8,192,256]{2,1,0:T(8,128)(2,1)} %copy.87), calls=%async_computation.3 | async-start | bytes 1572864 | tf_op jit(solution)/shard_map/all_to_all | solution.py:47
  87.8 17.5 %all-to-all-done.3 = bf16[8,192,256]{2,1,0:T(8,128)(2,1)S(1)} async-done(((bf16[8,192,256]{2,1,0:T(8,128)(2,1)}), bf16[8,192,256]{2,1,0:T(8,128)(2,1)S(1)}, u32[]{:S(2)}, u32[]{:S(2)}) %all-to-all-start.3) | async-done | bytes 786464 | tf_op jit(solution)/shard_map/all_to_all | solution.py:47
  105.3 0.1 copy.96
  105.4 0.5 copy.89
  106.0 9.6 %scatter_custom_fusion = bf16[192,2048]{0,1:T(8,128)(2,1)S(1)} fusion(s32[2048]{0:T(1024)S(1)} %bitcast.145, bf16[2048,192]{1,0:T(8,128)(2,1)S(1)} %copy.89, bf16[]{:T(256)} %constant.5.clone.1), kind=kCustom, calls=%fused_computation.24 | custom fusion | bytes 786434 | tf_op jit(solution)/shard_map/scatter | solution.py:50
  115.5 1.2 %copy.90 = bf16[192,2048]{1,0:T(8,128)(2,1)} copy(bf16[192,2048]{0,1:T(8,128)(2,1)S(1)} %scatter_custom_fusion) | data formatting | bytes 1572864 | tf_op jit(solution)/shard_map/scatter | solution.py:50
  (33 shorter events, 0.2 us)
Async XLA Ops:
  0.0 1.1 copy-start
  0.0 7.5 %copy-start.10 = (s32[1,1024]{1,0:T(1,128)S(1)}, s32[1,1024]{1,0:T(1,128)}, u32[]{:S(2)}) copy-start(s32[1,1024]{1,0:T(1,128)} %param.13) | copy-start | bytes 12292
  0.0 7.5 %copy-start.11 = (s32[1,20]{1,0:T(1,128)S(1)}, s32[1,20]{1,0:T(1,128)}, u32[]{:S(2)}) copy-start(s32[1,20]{1,0:T(1,128)} %param.12) | copy-start | bytes 244
  3.3 10.2 %all-to-all-start = ((bf16[4,64,512]{2,1,0:T(8,128)(2,1)}), bf16[4,64,512]{2,1,0:T(8,128)(2,1)S(1)}, u32[]{:S(2)}, u32[]{:S(2)}) async-start(bf16[4,64,512]{2,1,0:T(8,128)(2,1)} %bitcast.2), calls=%async_computation | async-start | bytes 524288 | tf_op jit(solution)/shard_map/all_to_all | solution.py:13
  7.5 37.4 %copy-start.6 = (s32[1024]{0:T(1024)}, s32[1024]{0:T(1024)S(1)}, u32[]{:S(2)}) copy-start(s32[1024]{0:T(1024)S(1)} %get-tuple-element.5) | copy-start | bytes 12292
  13.5 0.7 copy-start.4
  14.2 17.2 %copy-start.1 = (bf16[1,20,256,256]{3,2,1,0:T(8,128)(2,1)S(1)}, bf16[1,20,256,256]{3,2,1,0:T(8,128)(2,1)}, u32[]{:S(2)}) copy-start(bf16[1,20,256,256]{3,2,1,0:T(8,128)(2,1)} %param.10) | copy-start | bytes 7864324
  23.2 9.0 %copy-start.7 = (s32[1,20]{1,0:T(1,128)S(1)}, s32[1,20]{1,0:T(1,128)}, u32[]{:S(2)}) copy-start(s32[1,20]{1,0:T(1,128)} %param.11) | copy-start | bytes 244
  24.9 13.8 %all-to-all-start.1 = ((bf16[64,8,128]{2,0,1:T(8,128)(2,1)}), bf16[64,8,128]{2,0,1:T(8,128)(2,1)S(1)}, u32[]{:S(2)}, u32[]{:S(2)}) async-start(bf16[64,8,128]{2,0,1:T(8,128)(2,1)} %copy.77), calls=%async_computation.1 | async-start | bytes 262144 | tf_op jit(solution)/shard_map/all_to_all | solution.py:40
  42.9 2.0 %copy-start.8 = (s32[1,20]{1,0:T(1,128)S(1)}, s32[1,20]{1,0:T(1,128)}, u32[]{:S(2)}) copy-start(s32[1,20]{1,0:T(1,128)} %param.11) | copy-start | bytes 244
  56.1 10.7 %all-to-all-start.2 = ((bf16[64,8,128]{2,0,1:T(8,128)(2,1)}), bf16[64,8,128]{2,0,1:T(8,128)(2,1)S(1)}, u32[]{:S(2)}, u32[]{:S(2)}) async-start(bf16[64,8,128]{2,0,1:T(8,128)(2,1)} %copy.82), calls=%async_computation.2 | async-start | bytes 262144 | tf_op jit(solution)/shard_map/all_to_all | solution.py:43
  71.1 2.0 %copy-start.9 = (s32[1,20]{1,0:T(1,128)S(1)}, s32[1,20]{1,0:T(1,128)}, u32[]{:S(2)}) copy-start(s32[1,20]{1,0:T(1,128)} %param.11) | copy-start | bytes 244
  73.1 1.6 %copy-start.2 = (bf16[64,2048]{1,0:T(8,128)(2,1)S(1)}, bf16[64,2048]{1,0:T(8,128)(2,1)}, u32[]{:S(2)}) copy-start(bf16[64,2048]{1,0:T(8,128)(2,1)} %divide_convert_fusion.1) | copy-start | bytes 786436
  73.1 1.6 %copy-start.3 = (bf16[4,8,8,512]{3,2,0,1:T(8,128)(2,1)S(1)}, bf16[4,8,8,512]{3,2,0,1:T(8,128)(2,1)}, u32[]{:S(2)}) copy-start(bf16[4,8,8,512]{3,2,0,1:T(8,128)(2,1)} %copy.93) | copy-start | bytes 786436
  82.9 4.8 %copy-start.5 = (s32[1,2048]{1,0:T(1,128)S(1)}, s32[1,2048]{1,0:T(1,128)}, u32[]{:S(2)}) copy-start(s32[1,2048]{1,0:T(1,128)} %param.15) | copy-start | bytes 24580
  84.2 21.1 %all-to-all-start.3 = ((bf16[8,192,256]{2,1,0:T(8,128)(2,1)}), bf16[8,192,256]{2,1,0:T(8,128)(2,1)S(1)}, u32[]{:S(2)}, u32[]{:S(2)}) async-start(bf16[8,192,256]{2,1,0:T(8,128)(2,1)} %copy.87), calls=%async_computation.3 | async-start | bytes 1572864 | tf_op jit(solution)/shard_map/all_to_all | solution.py:47
